TPU v7x, 128 devices: a whole 4x4x4 slice. The times are simulated.
128 devices in a mesh: wide: 32 (over y_lo, x, z), narrow: 4 (over y_hi, core).
Axes of the slice: x: 4, y: 4 (y_hi: 2, y_lo: 2; y = y_hi * 2 + y_lo), z: 4, core: 2. Of those that a mesh axis runs over, the one named last changes fastest.
Arguments:
- pos_factor: float32 [1024, 131072], P('wide', 'narrow'), may hold values from -6 to 6
- vel_factor: float32 [1024, 131072], P('wide', 'narrow'), may hold values from -6 to 6
- stiff_vals: float32 [4, 512, 64, 256], P('narrow', 'wide'), may hold values from -0.375 to 0.375
- stiff_pattern: int32 [4, 512, 4], P('narrow', 'wide'), may hold values from 0 to 19
- mass_vals: float32 [4, 512, 64, 256], P('narrow', 'wide'), may hold values from -0.375 to 0.375
- mass_pattern: int32 [4, 512, 4], P('narrow', 'wide'), may hold values from 0 to 19
- interface: int32 [4, 32, 2, 2], P('narrow', 'wide'), may hold values from 0 to 15
Outputs:
- cross_tiles: float32 [1024, 1024], P(('wide', 'narrow'))
All inputs are finite; a program needn't handle non-finite values.
Results may differ from a plain program's by a relative error of at most 0.0001.
Values sent between devices are 32-bit elements; how exact they have to be, the bound alone decides.
A program may use at most 128 MiB of HBM per device.

v0:
```python
import math

import jax
import jax.numpy as jnp
from jax import lax
from jax.sharding import PartitionSpec as P


def from_behind(x, axis, by):
    size = lax.axis_size(axis)
    pairs = [(i, i + by) for i in range(size) if 0 <= i + by < size]
    return lax.ppermute(x, axis, pairs)


def fetch_rims(upward, downward):
    lower = from_behind(upward, "narrow", 1)
    upper = from_behind(downward, "narrow", -1)
    return (lower, upper)


def apply_block_matrix(values, pattern, extended):
    block_size = values.shape[1]
    total = jnp.zeros((extended.shape[0], values.shape[0], block_size), jnp.float32)
    for k in range(pattern.shape[1]):
        coupled = values[:, :, k * block_size : (k + 1) * block_size]
        picked = jnp.take(extended, pattern[:, k], axis=1)
        total = total + jnp.einsum("rbj,bij->rbi", picked, coupled, precision=lax.Precision.HIGHEST)
    return total.reshape(extended.shape[0], -1)


def shards(pos_factor, vel_factor, stiff_vals, stiff_pattern, mass_vals, mass_pattern, interface):
    block_count = stiff_vals.shape[1]
    block_size = stiff_vals.shape[2]
    stiff = stiff_vals[0]
    mass = mass_vals[0]
    stiff_idx = stiff_pattern[0]
    mass_idx = mass_pattern[0]
    picks = interface[0, 0]

    def as_blocks(field):
        return field.reshape(field.shape[0], block_count, block_size)

    pos_rows, vel_rows = (
        lax.all_to_all(pos_factor, "wide", split_axis=1, concat_axis=0, tiled=True),
        lax.all_to_all(vel_factor, "wide", split_axis=1, concat_axis=0, tiled=True),
    )
    pos_b = as_blocks(pos_rows)
    vel_b = as_blocks(vel_rows)
    upward = jnp.stack([jnp.take(pos_b, picks[0], axis=1), jnp.take(vel_b, picks[0], axis=1)], 0)
    downward = jnp.stack([jnp.take(pos_b, picks[1], axis=1), jnp.take(vel_b, picks[1], axis=1)], 0)
    lower, upper = fetch_rims(upward, downward)
    moved = apply_block_matrix(stiff, stiff_idx, jnp.concatenate([lower[0], pos_b, upper[0]], 1))
    velocity_local = apply_block_matrix(
        mass, mass_idx, jnp.concatenate([lower[1], vel_b, upper[1]], 1)
    )
    scale = 1.0 / math.sqrt(moved.shape[1] * lax.axis_size("wide") * lax.axis_size("narrow"))
    product = lax.dot_general(
        moved,
        velocity_local,
        (((1,), (1,)), ((), ())),
        precision=lax.Precision.HIGHEST,
        preferred_element_type=jnp.float32,
    )
    return lax.psum_scatter(product * scale, ("wide", "narrow"), scatter_dimension=0, tiled=True)


def solution(mesh):
    return jax.shard_map(
        shards,
        mesh=mesh,
        in_specs=(
            P("wide", "narrow"),
            P("wide", "narrow"),
            P("narrow", "wide", None, None),
            P("narrow", "wide", None),
            P("narrow", "wide", None, None),
            P("narrow", "wide", None),
            P("narrow", "wide", None, None),
        ),
        out_specs=P(("wide", "narrow"), None),
        check_vma=False,
    )
```

profile of v0, /device:TPU:0, one launch (start us, length us, event | category | flops | bytes accessed | tf_op | source)
XLA Modules:
  0.0 956.9 jit_solution(16257981143683502110)
XLA Ops:
  6.5 4.8 copy.23
  11.3 9.4 all-to-all-start
  20.8 4.8 copy.22
  25.5 52.1 %all-to-all-done = f32[32,32,1024]{2,0,1:T(8,128)} async-done(((f32[32,32,1024]{2,0,1:T(8,128)}), f32[32,32,1024]{2,0,1:T(8,128)}, u32[]{:S(2)}, u32[]{:S(2)}) %all-to-all-start) | async-done | bytes 4194336 | tf_op jit(solution)/shard_map/all_to_all | solution.py:44
  77.6 7.8 all-to-all-start.1
  85.5 0.0 reduce-scatter.2.cloned.1.call-start
  85.5 0.0 copy-done.13
  85.6 7.3 reshape.30
  92.8 6.8 copy.11
  99.6 2.8 gather_fusion.2
  102.4 2.8 gather_fusion
  105.2 35.2 %all-to-all-done.1 = f32[32,32,1024]{2,0,1:T(8,128)} async-done(((f32[32,32,1024]{2,0,1:T(8,128)}), f32[32,32,1024]{2,0,1:T(8,128)}, u32[]{:S(2)}, u32[]{:S(2)}) %all-to-all-start.1) | async-done | bytes 4194336 | tf_op jit(solution)/shard_map/all_to_all | solution.py:45
  140.4 7.3 reshape.31
  147.6 6.9 copy.13
  154.5 2.8 gather_fusion.3
  157.3 2.8 gather_fusion.1
  160.1 0.0 copy-start.11
  160.1 0.0 copy-start.12
  160.1 0.4 select_bitcast_fusion.1
  160.5 0.0 copy-start.7
  160.5 0.1 pad_maximum_fusion.2
  160.6 1.6 collective-permute-start
  162.3 0.1 pad_maximum_fusion.3
  162.4 1.3 collective-permute-start.1
  163.7 0.0 copy-done.11
  163.7 0.0 copy-done.12
  163.8 0.7 collective-permute-done
  164.5 0.1 slice_bitcast_fusion.3
  164.6 5.4 collective-permute-done.1
  170.0 0.1 slice_bitcast_fusion.2
  170.1 0.0 copy-done.7
  170.1 2.8 pad_maximum_fusion.1
  172.9 5.3 gather_fusion.11
  178.2 5.3 gather_fusion.10
  183.4 5.3 gather_fusion.9
  188.7 5.3 gather_fusion.8
  194.0 5.3 pad_maximum_fusion
  199.4 5.3 gather_fusion.7
  204.6 5.3 gather_fusion.6
  209.9 5.3 gather_fusion.5
  215.1 5.4 gather_fusion.4
  220.5 0.0 copy-done.8
  220.5 6.1 fusion.2
  226.6 0.0 copy-done.2
  226.6 0.0 copy-start.3
  226.6 4.1 fusion.4
  230.8 0.0 copy-done.3
  230.8 0.0 copy-start
  230.8 5.7 fusion.8
  236.5 0.0 copy-done
  236.5 5.7 fusion.6
  242.2 0.0 copy-done.4
  242.2 0.0 copy-done.9
  242.2 5.9 fusion.11
  248.0 0.0 copy-done.5
  248.0 5.6 fusion.13
  253.6 0.0 copy-done.6
  253.6 5.7 fusion.17
  259.3 0.0 copy-done.1
  259.3 5.6 fusion.15
  264.9 0.0 copy-done.10
  264.9 22.5 %bitcast_multiply_fusion = f32[1024,1024]{1,0:T(8,128)} fusion(f32[16,1024,64]{1,2,0:T(8,128)S(1)} %fusion.2, f32[16,1024,64]{1,2,0:T(8,128)S(1)} %fusion.4, f32[16,1024,64]{1,2,0:T(8,128)S(1)} %copy-done.10, f32[16,1024,64]{1,2,0:T(8,128)} %fusion.6, f32[16,1024,64]{1,2,0:T(8,128)} %fusion.11, f32[16,1024,64]{1,2,0:T(8,128)} %fusion.13, ...), kind=kOutput, calls=%fused_computation.16 | convolution fusion | flops 12892241920 | bytes 37748736 | tf_op jit(solution)/shard_map/dot_general | solution.py:57
  287.4 0.0 reduce-scatter.2.cloned.1.call-update
  287.5 662.6 %reduce-scatter.2.cloned.1.call-done = f32[8,1024]{1,0:T(8,128)} async-done(((f32[1024,1024]{1,0:T(8,128)}), f32[8,1024]{1,0:T(8,128)}) %reduce-scatter.2.cloned.1.call-update) | async-done | bytes 32784 | tf_op jit(solution)/shard_map/reduce_scatter | solution.py:64
  (18 shorter events, 0.1 us)
Async XLA Ops:
  11.3 66.3 %all-to-all-start = ((f32[32,32,1024]{2,0,1:T(8,128)}), f32[32,32,1024]{2,0,1:T(8,128)}, u32[]{:S(2)}, u32[]{:S(2)}) async-start(f32[32,32,1024]{2,0,1:T(8,128)} %bitcast.105), calls=%async_computation | async-start | bytes 8388608 | tf_op jit(solution)/shard_map/all_to_all | solution.py:44
  77.6 7.9 copy-start.13
  77.6 62.8 %all-to-all-start.1 = ((f32[32,32,1024]{2,0,1:T(8,128)}), f32[32,32,1024]{2,0,1:T(8,128)}, u32[]{:S(2)}, u32[]{:S(2)}) async-start(f32[32,32,1024]{2,0,1:T(8,128)} %bitcast.104), calls=%async_computation.1 | async-start | bytes 8388608 | tf_op jit(solution)/shard_map/all_to_all | solution.py:45
  85.5 864.6 %reduce-scatter.2.cloned.1.call-start = ((), (), s32[]{:S(2)}) async-start(), calls=%async_computation.3 | async-start | bytes 4227072 | tf_op jit(solution)/shard_map/reduce_scatter | solution.py:64
  160.1 3.6 copy-start.11
  160.1 3.6 copy-start.12
  160.5 9.6 copy-start.7
  160.6 3.8 collective-permute-start
  162.4 7.6 collective-permute-start.1
  215.1 5.4 copy-start.8
  220.5 6.1 copy-start.2
  226.6 4.2 copy-start.3
  230.8 5.7 copy-start
  236.5 5.7 copy-start.4
  236.5 5.7 copy-start.9
  242.2 5.9 copy-start.5
  248.0 5.6 copy-start.6
  253.6 5.7 copy-start.1
  259.3 5.6 copy-start.10
Sparse Core Ops, SparseCore 0:
  287.6 662.4 reduce-scatter.1
where the time goes:
time: 958 us; the launch traced here: 957 us
  waiting for transfers between devices  756 us (79%)
  local copies, waits for them, and re-layouts  91.5 us (10%)
  matrix products  66.8 us (7%)
  starting transfers between devices  20.2 us (2%)
  between operations  13.7 us (1%)
    reduce_scatter x1, waiting for transfers between devices, shards(): lax.psum_scatter(product * scale, ('wide', 'narrow'), scatter_dimension=0...  663 us
    all_to_all x1, waiting for transfers between devices, shards(): lax.all_to_all(pos_factor, 'wide', split_axis=1, concat_axis=0, tiled=True)  52.1 us
    dot_general x8, matrix products, apply_block_matrix(): jnp.einsum('rbj,bij->rbi', picked, coupled, precision=lax.Precision.HIGHEST)  44.3 us
    gather x8, local copies, waits for them, and re-layouts, apply_block_matrix(): picked = jnp.take(extended, pattern[:, k], axis=1)  42.3 us
    all_to_all x1, waiting for transfers between devices, shards(): lax.all_to_all(vel_factor, 'wide', split_axis=1, concat_axis=0, tiled=True)  35.2 us
    reshape x4, local copies, waits for them, and re-layouts, as_blocks(): return field.reshape(field.shape[0], block_count, block_size)  28.2 us
    dot_general x1, matrix products, shards(): lax.dot_general(moved, velocity_local, (((1,), (1,)), ((), ())), precisio...  22.5 us
  transfers between devices with their start and end apart: 5, of which 5 were waited for; matrix products, arithmetic and copies ran while one was open for 3% of the time, Pallas kernels for 0%

commit v1 on v0

v1 whole, which is shorter than its diff:
```python
import functools
import math

import jax
import jax.numpy as jnp
from jax import lax
from jax.experimental import pallas as pl
from jax.experimental.pallas import tpu as pltpu
from jax.sharding import PartitionSpec as P

MESH = pl.DeviceIdType.MESH
X_SIDE = 4
Z_SIDE = 4
LANES = 128

PAIRS = (
    (1, 1), (2, 3), (0, 2), (3, 0),
    (3, 3), (1, 2), (0, 1), (2, 0),
    (2, 2), (3, 1), (0, 3), (1, 0),
    (1, 3), (2, 1), (3, 2), (0, 0),
)
SHIFTS = tuple((dy, dx, dz) for dx, dz in PAIRS for dy in (0, 1))
CHUNK = 8


def two_halves(value):
    high = value.astype(jnp.bfloat16)
    low = (value - high.astype(jnp.float32)).astype(jnp.bfloat16)
    return high, low


def dot_t(a, b):
    return lax.dot_general(a, b, (((1,), (1,)), ((), ())), preferred_element_type=jnp.float32)


def dot3(ah, al, bh, bl):
    return dot_t(ah, bh) + (dot_t(ah, bl) + dot_t(al, bh))


def kernel(
    scale, pos_ref, vel_ref, stiff_ref, stiff_pat, mass_ref, mass_pat, picks, out_ref,
    pos_in, vel_in, halo, halo_out, stiff_h, stiff_l, mass_h, mass_l, e_h, e_l, p_f, p_h, p_l, v_h, v_l,
    x_out, x_in, y_out, y_in, z_out, z_in,
    send_sem, recv_sem, own_sem, halo_send, halo_recv, x_send, x_recv, y_send, y_recv, z_send, z_recv,
):
    wide = lax.axis_index("wide")
    narrow = lax.axis_index("narrow")
    plane = X_SIDE * Z_SIDE
    me_y, me_x, me_z = wide // plane, (wide // Z_SIDE) % X_SIDE, wide % Z_SIDE
    core, high_y = narrow % 2, narrow // 2
    slots = len(SHIFTS)
    chunks = slots // CHUNK
    cols, dofs = pos_in.shape[1], pos_in.shape[2]
    rows = CHUNK * cols
    blocks = mass_ref.shape[1]
    size = mass_ref.shape[2]

    def to(shift):
        dy, dx, dz = shift
        return ((me_y + dy) % 2) * plane + ((me_x + dx) % X_SIDE) * Z_SIDE + (me_z + dz) % Z_SIDE

    def back(shift):
        dy, dx, dz = shift
        return to((dy, (X_SIDE - dx) % X_SIDE, (Z_SIDE - dz) % Z_SIDE))

    core_partner = {"narrow": narrow + 1 - 2 * core}
    y_partner = {"wide": (wide + plane) % (2 * plane), "narrow": (narrow + 2) % 4}

    barrier = pltpu.get_barrier_semaphore()
    for shift in SHIFTS:
        if shift != (0, 0, 0):
            pl.semaphore_signal(barrier, inc=1, device_id={"wide": to(shift)}, device_id_type=MESH)
    for step in (1, 2, 3):
        pl.semaphore_signal(barrier, inc=1, device_id={"narrow": (narrow + step) % 4}, device_id_type=MESH)
    pl.semaphore_signal(barrier, inc=1, device_id=y_partner, device_id_type=MESH)
    pl.semaphore_wait(barrier, slots - 1 + 3 + 1)

    def exchange(which, slot):
        shift = SHIFTS[slot]
        source = (vel_ref, pos_ref)[which]
        target = to(shift)
        view = source.at[:, pl.ds(pl.multiple_of(target * dofs, dofs), dofs)]
        into = vel_in.at[wide] if which == 0 else pos_in.at[slot]
        if shift == (0, 0, 0):
            return pltpu.make_async_copy(view, into, own_sem.at[which])
        return pltpu.make_async_remote_copy(
            src_ref=view, dst_ref=into, send_sem=send_sem.at[which, slot], recv_sem=recv_sem.at[which, slot],
            device_id={"wide": target}, device_id_type=MESH,
        )

    copies = [[exchange(which, slot) for slot in range(slots)] for which in range(2)]
    for group in copies:
        for copy in group:
            copy.start()

    def arrived(which, slot):
        copy = copies[which][slot]
        if SHIFTS[slot] == (0, 0, 0):
            copy.wait()
        else:
            copy.wait_recv()

    lane = lax.broadcasted_iota(jnp.int32, (1, LANES), 1)
    left = lane < size
    half = lane // size

    def build(values, pattern, into_h, into_l):
        def row(b, carry):
            tiles = [values[0, b, :, t * LANES:(t + 1) * LANES] for t in range(2)]
            turned = [pltpu.roll(t, size, 1) for t in tiles]
            twice = []
            for t in range(2):
                twice.append(jnp.where(left, tiles[t], turned[t]))
                twice.append(jnp.where(left, turned[t], tiles[t]))
            at = pl.ds(pl.multiple_of(b * size, size), size)
            for pair in range(into_h.shape[1] // LANES):
                total = jnp.zeros((size, LANES), jnp.float32)
                for k in range(4):
                    total = total + jnp.where(half == pattern[0, b, k] - 2 * pair, twice[k], 0.0)
                h, l = two_halves(total)
                into_h[at, pair * LANES:(pair + 1) * LANES] = h
                into_l[at, pair * LANES:(pair + 1) * LANES] = l
            return carry

        lax.fori_loop(0, blocks, row, 0)

    build(mass_ref, mass_pat, mass_h, mass_l)
    build(stiff_ref, stiff_pat, stiff_h, stiff_l)

    @pl.when(narrow == 0)
    def _():
        halo[:, 0] = jnp.zeros(halo.shape[:1] + halo.shape[2:], jnp.float32)

    @pl.when(narrow == 3)
    def _():
        halo[:, 1] = jnp.zeros(halo.shape[:1] + halo.shape[2:], jnp.float32)

    wanted = [jnp.where(left, picks[0, 0, way, 0], picks[0, 0, way, 1]) for way in range(2)]

    def pick(field, which, q):
        def one(i, carry):
            found = [jnp.zeros((cols, LANES), jnp.float32)] * 2
            for t in range(dofs // LANES):
                tile = field[q * CHUNK + i, :, t * LANES:(t + 1) * LANES]
                turned = pltpu.roll(tile, size, 1)
                twice = (jnp.where(left, tile, turned), jnp.where(left, turned, tile))
                for way in range(2):
                    for h in range(2):
                        found[way] = jnp.where(wanted[way] == 2 * t + h, twice[h], found[way])
            for way in range(2):
                halo_out[which, way, q, pl.ds(pl.multiple_of(i * cols, cols), cols)] = found[way]
            return carry
        lax.fori_loop(0, CHUNK, one, 0)

    def halo_copy(which, q, way):
        return pltpu.make_async_remote_copy(
            src_ref=halo_out.at[which, way, q], dst_ref=halo.at[which, way, q],
            send_sem=halo_send.at[which, way, q], recv_sem=halo_recv.at[which, way, q],
            device_id={"narrow": (narrow + (1 if way == 0 else 3)) % 4}, device_id_type=MESH,
        )

    def send_halo(field, which, q):
        pick(field, which, q)
        for way in range(2):
            @pl.when(narrow != (3 if way == 0 else 0))
            def _():
                halo_copy(which, q, way).start()

    def take_halo(which, q):
        for way in range(2):
            @pl.when(narrow != (0 if way == 0 else 3))
            def _():
                halo_copy(which, q, way).wait_recv()

    def drain_halo(which, q):
        for way in range(2):
            @pl.when(narrow != (3 if way == 0 else 0))
            def _():
                halo_copy(which, q, way).wait_send()

    def split_own(field, q):
        def one(i, carry):
            h, l = two_halves(field[q * CHUNK + i])
            at = pl.ds(pl.multiple_of(i * cols, cols), cols)
            e_h[at, LANES:LANES + dofs] = h
            e_l[at, LANES:LANES + dofs] = l
            return carry
        lax.fori_loop(0, CHUNK, one, 0)

    def split_halo(which, q):
        for way in range(2):
            h, l = two_halves(halo[which, way, q])
            at = slice(0, LANES) if way == 0 else slice(LANES + dofs, LANES + dofs + LANES)
            e_h[:, at] = h
            e_l[:, at] = l

    tile = 256

    def apply_own(into_h, into_l):
        def one(j, carry):
            at = pl.ds(pl.multiple_of(j * tile, tile), tile)
            mid = slice(LANES, LANES + dofs)
            p_f[:, at] = dot3(e_h[:, mid], e_l[:, mid], into_h[at, mid], into_l[at, mid])
            return carry
        lax.fori_loop(0, dofs // tile, one, 0)

    def apply_halo(into_h, into_l, done):
        def one(j, carry):
            at = pl.ds(pl.multiple_of(j * tile, tile), tile)
            total = p_f[:, at]
            for side in (slice(0, LANES), slice(LANES + dofs, LANES + dofs + LANES)):
                total = total + dot3(e_h[:, side], e_l[:, side], into_h[at, side], into_l[at, side])
            h, l = two_halves(total)
            done(at, h, l)
            return carry
        lax.fori_loop(0, dofs // tile, one, 0)

    for slot in range(slots):
        arrived(0, slot)
    for q in range(chunks):
        send_halo(vel_in, 0, q)
    for q in range(chunks):
        split_own(vel_in, q)
        apply_own(mass_h, mass_l)
        take_halo(0, q)
        split_halo(0, q)
        at_rows = slice(q * rows, (q + 1) * rows)

        def keep_v(at, h, l):
            v_h[at_rows, at] = h
            v_l[at_rows, at] = l
        apply_halo(mass_h, mass_l, keep_v)

    def core_copy(q):
        return pltpu.make_async_remote_copy(
            src_ref=x_out.at[1 - core, q], dst_ref=x_in.at[q], send_sem=x_send.at[q], recv_sem=x_recv.at[q],
            device_id=core_partner, device_id_type=MESH,
        )

    def y_copy(q):
        return pltpu.make_async_remote_copy(
            src_ref=y_out.at[1 - high_y, q], dst_ref=y_in.at[q], send_sem=y_send.at[q], recv_sem=y_recv.at[q],
            device_id=y_partner, device_id_type=MESH,
        )

    def z_copy(slot):
        return pltpu.make_async_remote_copy(
            src_ref=z_out.at[slot], dst_ref=z_in.at[slot], send_sem=z_send.at[slot], recv_sem=z_recv.at[slot],
            device_id={"wide": back(SHIFTS[slot])}, device_id_type=MESH,
        )

    def products(q):
        for slot in range(q * CHUNK, (q + 1) * CHUNK):
            arrived(1, slot)
        send_halo(pos_in, 1, q)
        split_own(pos_in, q)
        apply_own(stiff_h, stiff_l)
        take_halo(1, q)
        split_halo(1, q)

        def keep_p(at, h, l):
            p_h[:, at] = h
            p_l[:, at] = l
        apply_halo(stiff_h, stiff_l, keep_p)

        def one(j, carry):
            at = pl.ds(pl.multiple_of(j * tile, tile), tile)
            x = dot3(p_h[...], p_l[...], v_h[at, :], v_l[at, :])
            x = x.reshape(CHUNK, 2, 2, 8, tile)
            for c in range(2):
                x_out[c, q, :, :, :, at] = x[:, :, c]
            return carry
        lax.fori_loop(0, v_h.shape[0] // tile, one, 0)
        core_copy(q).start()

    def reduce_core(q):
        core_copy(q).wait_recv()

        def one(i, carry):
            for h in range(2):
                y_out[h, q, i] = x_out[core, q, i, h] + x_in[q, i, h]
            return carry
        lax.fori_loop(0, CHUNK, one, 0)
        y_copy(q).start()

    def reduce_y(q):
        y_copy(q).wait_recv()
        for i in range(CHUNK):
            slot = q * CHUNK + i
            z_out[slot] = y_out[high_y, q, i] + y_in[q, i ^ 1]
            if SHIFTS[slot] != (0, 0, 0):
                z_copy(slot).start()

    for q in range(chunks):
        products(q)
        reduce_core(q)
        reduce_y(q)

    home = SHIFTS.index((0, 0, 0))
    total = z_out[home]
    for slot in range(slots):
        if slot != home:
            z_copy(slot).wait_recv()
            total = total + z_in[slot]
    out_ref[...] = total * scale

    for group in copies:
        for slot in range(slots):
            if slot != home:
                group[slot].wait_send()
    for which in range(2):
        for q in range(chunks):
            drain_halo(which, q)
    for q in range(chunks):
        core_copy(q).wait_send()
        y_copy(q).wait_send()
    for slot in range(slots):
        if slot != home:
            z_copy(slot).wait_send()


def shards(pos_factor, vel_factor, stiff_vals, stiff_pattern, mass_vals, mass_pattern, interface):
    wide, narrow = lax.axis_size("wide"), lax.axis_size("narrow")
    cols = pos_factor.shape[0]
    dofs = pos_factor.shape[1] // wide
    every = cols * wide
    slots = len(SHIFTS)
    chunks = slots // CHUNK
    rows = CHUNK * cols
    extended = dofs + 2 * LANES
    scale = 1.0 / math.sqrt(dofs * wide * narrow)
    f32, b16 = jnp.float32, jnp.bfloat16
    vmem = functools.partial(pl.BlockSpec, memory_space=pltpu.VMEM)
    smem = functools.partial(pl.BlockSpec, memory_space=pltpu.SMEM)
    hbm = functools.partial(pl.BlockSpec, memory_space=pl.ANY)
    dma = pltpu.SemaphoreType.DMA
    return pl.pallas_call(
        functools.partial(kernel, scale),
        out_shape=jax.ShapeDtypeStruct((8, every), f32),
        in_specs=[hbm(), hbm(), vmem(), smem(), vmem(), smem(), smem()],
        out_specs=vmem(),
        scratch_shapes=[
            pltpu.VMEM((slots, cols, dofs), f32),
            pltpu.VMEM((slots, cols, dofs), f32),
            pltpu.VMEM((2, 2, chunks, rows, LANES), f32),
            pltpu.VMEM((2, 2, chunks, rows, LANES), f32),
            pltpu.VMEM((dofs, extended), b16),
            pltpu.VMEM((dofs, extended), b16),
            pltpu.VMEM((dofs, extended), b16),
            pltpu.VMEM((dofs, extended), b16),
            pltpu.VMEM((rows, extended), b16),
            pltpu.VMEM((rows, extended), b16),
            pltpu.VMEM((rows, dofs), f32),
            pltpu.VMEM((rows, dofs), b16),
            pltpu.VMEM((rows, dofs), b16),
            pltpu.VMEM((every, dofs), b16),
            pltpu.VMEM((every, dofs), b16),
            pltpu.VMEM((2, chunks, CHUNK, 2, 8, every), f32),
            pltpu.VMEM((chunks, CHUNK, 2, 8, every), f32),
            pltpu.VMEM((2, chunks, CHUNK, 8, every), f32),
            pltpu.VMEM((chunks, CHUNK, 8, every), f32),
            pltpu.VMEM((slots, 8, every), f32),
            pltpu.VMEM((slots, 8, every), f32),
            dma((2, slots)), dma((2, slots)), dma((2,)),
            dma((2, 2, chunks)), dma((2, 2, chunks)),
            dma((chunks,)), dma((chunks,)),
            dma((chunks,)), dma((chunks,)),
            dma((slots,)), dma((slots,)),
        ],
        compiler_params=pltpu.CompilerParams(
            collective_id=0, has_side_effects=True, vmem_limit_bytes=60 << 20
        ),
    )(pos_factor, vel_factor, stiff_vals, stiff_pattern, mass_vals, mass_pattern, interface)


def solution(mesh):
    return jax.shard_map(
        shards,
        mesh=mesh,
        in_specs=(
            P("wide", "narrow"),
            P("wide", "narrow"),
            P("narrow", "wide", None, None),
            P("narrow", "wide", None),
            P("narrow", "wide", None, None),
            P("narrow", "wide", None),
            P("narrow", "wide", None, None),
        ),
        out_specs=P(("wide", "narrow"), None),
        check_vma=False,
    )
```

time: 958 us -> 218 us (0.23)
  waiting for transfers between devices: 756 us -> 0 us
  Pallas kernels: 0 us -> 211 us
  local copies, waits for them, and re-layouts: 91.5 us -> 4.08 us
  matrix products: 66.8 us -> 0 us
  starting transfers between devices: 20.2 us -> 0 us
  between operations: 13.7 us -> 0.01 us
    reduce_scatter x1 -> x0, waiting for transfers between devices: 663 us -> none  [shards(): lax.psum_scatter(product * scale, ('wide', 'narrow'), scatter_dimension=0...]
    pallas_call x0 -> x1, Pallas kernels: none -> 211 us  [shards(): pl.pallas_call(functools.partial(kernel, scale), out_shape=jax.ShapeDtype...]
    all_to_all x2 -> x0, waiting for transfers between devices: 87.3 us -> none  [the longest x1 52.1 us: shards(): lax.all_to_all(pos_factor, 'wide', split_axis=1, concat_axis=0, tiled=True)]
    dot_general x9 -> x0, matrix products: 66.8 us -> none  [the longest x8 44.3 us: apply_block_matrix(): jnp.einsum('rbj,bij->rbi', picked, coupled, precision=lax.Precision.HIGHEST)]
    gather x12 -> x0, local copies, waits for them, and re-layouts: 53.4 us -> none  [the longest x8 42.3 us: apply_block_matrix(): picked = jnp.take(extended, pattern[:, k], axis=1)]
    reshape x4 -> x0, local copies, waits for them, and re-layouts: 28.2 us -> none  [as_blocks(): return field.reshape(field.shape[0], block_count, block_size)]
    all_to_all x2 -> x0, starting transfers between devices: 17.3 us -> none  [the longest x1 9.41 us: shards(): lax.all_to_all(pos_factor, 'wide', split_axis=1, concat_axis=0, tiled=True)]
  transfers between devices with their start and end apart: 5 -> 0, of which waited for: 5 -> 0; matrix products, arithmetic and copies ran while one was open for 3% -> 0% of each run, Pallas kernels for 0% -> 0%
where the time goes in v1:
time: 218 us; the launch traced here: 215 us
  Pallas kernels  211 us (97%)
  local copies, waits for them, and re-layouts  4.08 us (2%)
    pallas_call x1, Pallas kernels, shards(): pl.pallas_call(functools.partial(kernel, scale), out_shape=jax.ShapeDtype...  211 us

profile of v1, /device:TPU:0, one launch (start us, length us, event | category | flops | bytes accessed | tf_op | source)
XLA Modules:
  0.0 215.4 jit_solution(1986637270869748017)
XLA Ops:
  0.0 1.4 copy.8.stiff_pat
  1.4 1.3 copy.9.mass_pat
  2.7 211.3 %shard_map.73 = f32[8,1024]{1,0:T(8,128)} custom-call(f32[32,32768]{1,0:T(8,128)} %pos_ref.1, f32[32,32768]{1,0:T(8,128)} %vel_ref.1, f32[1,16,64,256]{3,2,1,0:T(8,128)} %stiff_ref.1, s32[1,16,4]{2,1,0:T(8,128)} %copy.8.stiff_pat, f32[1,16,64,256]{3,2,1,0:T(8,128)} %mass_ref.1, s32[1,16,4]{2,1,0:T(8,128)} %copy.9.mass_pat, s32[1,1,2,2]{3,2,1,0:T(2,128)} %picks.1), custom_call_target="tpu_custom_call" | custom-call | tf_op jit(solution)/shard_map/pallas_call | solution.py:337
  214.0 1.4 copy.11

commit v2 on v0

v2 whole, which is shorter than its diff:
```python
import functools
import math

import jax
import jax.numpy as jnp
from jax import lax
from jax.experimental import pallas as pl
from jax.experimental.pallas import tpu as pltpu
from jax.sharding import PartitionSpec as P

MESH = pl.DeviceIdType.MESH
X_SIDE = 4
Z_SIDE = 4
LANES = 128

PAIRS = (
    (1, 1), (3, 3), (2, 0), (0, 2),
    (1, 3), (3, 1), (2, 2), (0, 0),
    (1, 2), (3, 2), (2, 1), (2, 3),
    (3, 0), (1, 0), (0, 3), (0, 1),
)
SHIFTS = tuple((dy, dx, dz) for dx, dz in PAIRS for dy in (0, 1))
CUTS = (0, 8, 16, 24, 32)
WINDOW = 8
LAG = 5
TILE = 256
HOME = SHIFTS.index((0, 0, 0))
NEGATED = tuple(SHIFTS.index((dy, -dx % X_SIDE, -dz % Z_SIDE)) for dy, dx, dz in SHIFTS)


def two_halves(value):
    high = value.astype(jnp.bfloat16)
    low = (value - high.astype(jnp.float32)).astype(jnp.bfloat16)
    return high, low


def dot_t(a, b):
    return lax.dot_general(a, b, (((1,), (1,)), ((), ())), preferred_element_type=jnp.float32)


def dot3(ah, al, bh, bl):
    return dot_t(ah, bh) + (dot_t(ah, bl) + dot_t(al, bh))


def kernel(
    scale, pos_ref, vel_ref, stiff_ref, stiff_pat, mass_ref, mass_pat, picks, out_ref,
    pos_in, vel_in, relay, halo, halo_out, stiff_h, stiff_l, mass_h, mass_l,
    ev_h, ev_l, ep_h, ep_l, v_f, p_f, p_h, p_l, v_h, v_l,
    x_out, x_in, y_out, y_in, z_out, z_in,
    send_sem, recv_sem, own_sem, relay_send, relay_recv, halo_send, halo_recv, x_send, x_recv, y_send, y_recv, z_send, z_recv,
):
    wide = lax.axis_index("wide")
    narrow = lax.axis_index("narrow")
    plane = X_SIDE * Z_SIDE
    me_y, me_x, me_z = wide // plane, (wide // Z_SIDE) % X_SIDE, wide % Z_SIDE
    core, high_y = narrow % 2, narrow // 2
    slots = len(SHIFTS)
    chunks = len(CUTS) - 1
    cols, dofs = pos_in.shape[1], pos_in.shape[2]
    every = slots * cols
    blocks = mass_ref.shape[1]
    size = mass_ref.shape[2]
    tiles = every // TILE

    def at_distance(dy, dx, dz):
        return ((me_y + dy) % 2) * plane + ((me_x + dx + X_SIDE) % X_SIDE) * Z_SIDE + (me_z + dz + Z_SIDE) % Z_SIDE

    sign = 1 - 2 * core

    def target_of(slot):
        dy, dx, dz = SHIFTS[slot]
        return at_distance(dy, sign * dx, sign * dz)

    def source_of(slot):
        dy, dx, dz = SHIFTS[slot]
        return at_distance(dy, -sign * dx, -sign * dz)

    core_partner = {"narrow": narrow + 1 - 2 * core}
    y_partner = {"wide": (wide + plane) % (2 * plane), "narrow": (narrow + 2) % 4}

    barrier = pltpu.get_barrier_semaphore()
    for slot in range(slots):
        if slot != HOME:
            pl.semaphore_signal(barrier, inc=1, device_id={"wide": target_of(slot)}, device_id_type=MESH)
    for step in (1, 2, 3):
        pl.semaphore_signal(barrier, inc=1, device_id={"narrow": (narrow + step) % 4}, device_id_type=MESH)
    pl.semaphore_signal(barrier, inc=1, device_id=y_partner, device_id_type=MESH)
    pl.semaphore_wait(barrier, slots - 1 + 3 + 1)

    pairs = len(PAIRS)
    here = HOME // 2

    def landing(which, slot, owner):
        return vel_in.at[owner] if which == 0 else pos_in.at[slot]

    def block_for(which, target):
        return (vel_ref, pos_ref)[which].at[:, pl.ds(pl.multiple_of(target * dofs, dofs), dofs)]

    across = (wide + plane) % (2 * plane)
    home_copies = [
        pltpu.make_async_copy(block_for(which, wide), landing(which, HOME, wide), own_sem.at[which]) for which in range(2)
    ]

    def along_y(which, k):
        return pltpu.make_async_remote_copy(
            src_ref=block_for(which, target_of(2 * k + 1)),
            dst_ref=landing(which, HOME + 1, wide) if k == here else relay.at[which, k],
            send_sem=relay_send.at[which, k], recv_sem=relay_recv.at[which, k],
            device_id={"wide": across}, device_id_type=MESH,
        )

    def in_plane(which, slot):
        k, far = slot // 2, slot % 2
        target = target_of(2 * k)
        return pltpu.make_async_remote_copy(
            src_ref=relay.at[which, k] if far else block_for(which, target),
            dst_ref=landing(which, slot, across if far else wide),
            send_sem=send_sem.at[which, slot], recv_sem=recv_sem.at[which, slot],
            device_id={"wide": target}, device_id_type=MESH,
        )

    def issue(n):
        if n < 2 * pairs:
            which, k = n // pairs, n % pairs
            along_y(which, k).start()
            if k != here:
                in_plane(which, 2 * k).start()

    def step(n):
        which, k = n // pairs, n % pairs
        along_y(which, k).wait_recv()
        if k != here:
            in_plane(which, 2 * k + 1).start()
        issue(n + WINDOW)

    for which in range(2):
        home_copies[which].start()
    for n in range(WINDOW):
        issue(n)

    def arrived(which, slot):
        if slot == HOME:
            home_copies[which].wait()
        elif slot // 2 != here:
            in_plane(which, slot).wait_recv()

    lane = lax.broadcasted_iota(jnp.int32, (1, LANES), 1)
    left = lane < size
    half = lane // size
    ends = (slice(0, LANES), slice(LANES + dofs, LANES + dofs + LANES))
    middle = slice(LANES, LANES + dofs)

    def build(values, pattern, into_h, into_l):
        def row(b, carry):
            pair_tiles = [values[0, b, :, t * LANES:(t + 1) * LANES] for t in range(2)]
            turned = [pltpu.roll(t, size, 1) for t in pair_tiles]
            twice = []
            for t in range(2):
                twice.append(jnp.where(left, pair_tiles[t], turned[t]))
                twice.append(jnp.where(left, turned[t], pair_tiles[t]))
            at = pl.ds(pl.multiple_of(b * size, size), size)
            for pair in range(into_h.shape[1] // LANES):
                total = jnp.zeros((size, LANES), jnp.float32)
                for k in range(4):
                    total = total + jnp.where(half == pattern[0, k, b] - 2 * pair, twice[k], 0.0)
                h, l = two_halves(total)
                into_h[at, pair * LANES:(pair + 1) * LANES] = h
                into_l[at, pair * LANES:(pair + 1) * LANES] = l
            return carry

        lax.fori_loop(0, blocks, row, 0)

    build(mass_ref, mass_pat, mass_h, mass_l)
    build(stiff_ref, stiff_pat, stiff_h, stiff_l)

    @pl.when(narrow == 0)
    def _():
        halo[:, 0] = jnp.zeros(halo.shape[:1] + halo.shape[2:], jnp.float32)

    @pl.when(narrow == 3)
    def _():
        halo[:, 1] = jnp.zeros(halo.shape[:1] + halo.shape[2:], jnp.float32)

    wanted = [jnp.where(left, picks[0, 0, way, 0], picks[0, 0, way, 1]) for way in range(2)]

    def take_in(which, field, entry, into_h, into_l, at):
        found = [jnp.zeros((cols, LANES), jnp.float32)] * 2
        for t in range(dofs // LANES):
            tile = field[entry, :, t * LANES:(t + 1) * LANES]
            turned = pltpu.roll(tile, size, 1)
            twice = (jnp.where(left, tile, turned), jnp.where(left, turned, tile))
            for way in range(2):
                for h in range(2):
                    found[way] = jnp.where(wanted[way] == 2 * t + h, twice[h], found[way])
            high, low = two_halves(tile)
            into_h[at, LANES + t * LANES:2 * LANES + t * LANES] = high
            into_l[at, LANES + t * LANES:2 * LANES + t * LANES] = low
        for way in range(2):
            halo_out[which, way, entry] = found[way]

    def halo_copy(which, q, way):
        lo, hi = (0, slots) if which == 0 else CUTS[q:q + 2]
        n = 0 if which == 0 else 1 + q
        return pltpu.make_async_remote_copy(
            src_ref=halo_out.at[which, way, lo:hi], dst_ref=halo.at[which, way, lo:hi],
            send_sem=halo_send.at[n, way], recv_sem=halo_recv.at[n, way],
            device_id={"narrow": (narrow + (1 if way == 0 else 3)) % 4}, device_id_type=MESH,
        )

    def send_halo(which, q):
        for way in range(2):
            @pl.when(narrow != (3 if way == 0 else 0))
            def _():
                halo_copy(which, q, way).start()

    def take_halo(which, q):
        for way in range(2):
            @pl.when(narrow != (0 if way == 0 else 3))
            def _():
                halo_copy(which, q, way).wait_recv()

    def drain_halo(which, q):
        for way in range(2):
            @pl.when(narrow != (3 if way == 0 else 0))
            def _():
                halo_copy(which, q, way).wait_send()

    def per_tile(count, body):
        def one(j, carry):
            body(j, pl.ds(pl.multiple_of(j * TILE, TILE), TILE))
            return carry
        lax.fori_loop(0, count, one, 0)

    def split_halo(which, entry, into_h, into_l, at):
        for way in range(2):
            into_h[at, ends[way]], into_l[at, ends[way]] = two_halves(halo[which, way, entry])

    def velocity_first(q):
        rows = slice(q * TILE, (q + 1) * TILE)

        def body(j, at):
            v_f[rows, at] = dot3(ev_h[rows, middle], ev_l[rows, middle], mass_h[at, middle], mass_l[at, middle])
        per_tile(dofs // TILE, body)

    def velocity_second():
        take_halo(0, 0)

        def one(i, carry):
            split_halo(0, i, ev_h, ev_l, pl.ds(pl.multiple_of(i * cols, cols), cols))
            return carry
        lax.fori_loop(0, slots, one, 0)

        def rows_of(q, carry):
            rows = pl.ds(pl.multiple_of(q * TILE, TILE), TILE)

            def body(j, at):
                total = v_f[rows, at]
                for side in ends:
                    total = total + dot3(ev_h[rows, side], ev_l[rows, side], mass_h[at, side], mass_l[at, side])
                v_h[rows, at], v_l[rows, at] = two_halves(total)
            per_tile(dofs // TILE, body)
            return carry
        lax.fori_loop(0, every // TILE, rows_of, 0)

    def core_copy(q, j):
        lo, hi = CUTS[q:q + 2]
        return pltpu.make_async_remote_copy(
            src_ref=x_out.at[1 - core, j, lo:hi], dst_ref=x_in.at[j, lo:hi],
            send_sem=x_send.at[q, j], recv_sem=x_recv.at[q, j], device_id=core_partner, device_id_type=MESH,
        )

    def y_copy(q, j):
        lo, hi = CUTS[q:q + 2]
        return pltpu.make_async_remote_copy(
            src_ref=y_out.at[1 - high_y, j, lo:hi], dst_ref=y_in.at[j, lo:hi],
            send_sem=y_send.at[q, j], recv_sem=y_recv.at[q, j], device_id=y_partner, device_id_type=MESH,
        )

    def z_copy(slot, j):
        at = slice(j * TILE, (j + 1) * TILE)
        return pltpu.make_async_remote_copy(
            src_ref=z_out.at[slot, :, at], dst_ref=z_in.at[slot, :, at],
            send_sem=z_send.at[slot, j], recv_sem=z_recv.at[slot, j],
            device_id={"wide": source_of(slot)}, device_id_type=MESH,
        )

    def rows_at(slot, end):
        return slice(slot * cols, end * cols)

    def position_in(slot):
        arrived(1, slot)
        take_in(1, pos_in, slot, ep_h, ep_l, rows_at(slot, slot + 1))

    def position_halo(q):
        take_halo(1, q)
        for slot in range(*CUTS[q:q + 2]):
            split_halo(1, NEGATED[slot], ep_h, ep_l, rows_at(slot, slot + 1))

    def position_first(q):
        rows = rows_at(*CUTS[q:q + 2])

        def body(j, at):
            p_f[:, at] = dot3(ep_h[rows, middle], ep_l[rows, middle], stiff_h[at, middle], stiff_l[at, middle])
        per_tile(dofs // TILE, body)

    def position_second(q):
        position_halo(q)
        lo, hi = CUTS[q:q + 2]
        rows, into = rows_at(lo, hi), rows_at(0, hi - lo)

        def body(j, at):
            total = p_f[:, at]
            for side in ends:
                total = total + dot3(ep_h[rows, side], ep_l[rows, side], stiff_h[at, side], stiff_l[at, side])
            p_h[into, at], p_l[into, at] = two_halves(total)
        per_tile(dofs // TILE, body)

    def product_tile(q, j, at):
        lo, hi = CUTS[q:q + 2]
        rows = rows_at(0, hi - lo)
        x = dot3(p_h[rows, :], p_l[rows, :], v_h[at, :], v_l[at, :])
        x = x.reshape(hi - lo, 2, 2, 8, TILE)
        for c in range(2):
            x_out[c, j, lo:hi] = x[:, :, c]
        core_copy(q, j).start()

    def core_tile(q, j):
        core_copy(q, j).wait_recv()
        for slot in range(*CUTS[q:q + 2]):
            for h in range(2):
                y_out[h, j, slot] = x_out[core, j, slot, h] + x_in[j, NEGATED[slot], h]
        y_copy(q, j).start()

    def products(q):
        per_tile(tiles, functools.partial(product_tile, q))

    def reduce_core(q):
        def one(j, carry):
            core_tile(q, j)
            return carry
        lax.fori_loop(0, tiles, one, 0)

    def products_and_reduce(q):
        def one(j, carry):
            product_tile(q, j, pl.ds(pl.multiple_of(j * TILE, TILE), TILE))

            @pl.when(j > 0)
            def _():
                core_tile(q, j - 1)
            return carry
        lax.fori_loop(0, tiles, one, 0)
        core_tile(q, tiles - 1)

    def reduce_y(q):
        for j in range(tiles):
            y_copy(q, j).wait_recv()
            for slot in range(*CUTS[q:q + 2]):
                z_out[slot, :, j * TILE:(j + 1) * TILE] = y_out[high_y, j, slot] + y_in[j, slot ^ 1]
                if slot != HOME:
                    z_copy(slot, j).start()

    def velocity_in(k):
        for slot in (2 * k, 2 * k + 1):
            arrived(0, slot)
            source = source_of(slot)
            take_in(0, vel_in, source, ev_h, ev_l, pl.ds(pl.multiple_of(source * cols, cols), cols))

    pending = list(range(2 * pairs))

    def steps(count):
        for _ in range(count):
            if pending:
                step(pending.pop(0))

    def chunk_in(q):
        for slot in range(*CUTS[q:q + 2]):
            position_in(slot)
        send_halo(1, q)

    steps(LAG)
    for k in range(pairs):
        steps(1)
        velocity_in(k)
    send_halo(0, 0)
    for q in range(every // TILE):
        velocity_first(q)
        steps(1)
    chunk_in(0)
    steps(2)
    velocity_second()
    steps(2)
    position_first(0)
    chunk_in(1)
    for q in range(2, chunks):
        steps(2)
        position_second(q - 2)
        products(q - 2)
        if q > 2:
            reduce_core(q - 3)
        steps(2)
        position_first(q - 1)
        chunk_in(q)
    steps(2 * pairs)
    last = chunks - 1
    position_second(last - 1)
    products(last - 1)
    reduce_core(last - 2)
    reduce_y(last - 3)
    position_first(last)
    reduce_core(last - 1)
    reduce_y(last - 2)
    position_second(last)
    products_and_reduce(last)
    reduce_y(last - 1)
    reduce_y(last)

    for j in range(tiles):
        at = slice(j * TILE, (j + 1) * TILE)
        total = z_out[HOME, :, at]
        for slot in range(slots):
            if slot != HOME:
                z_copy(slot, j).wait_recv()
                total = total + z_in[slot, :, at]
        out_ref[:, at] = total * scale

    for which in range(2):
        for k in range(pairs):
            along_y(which, k).wait_send()
            if k != here:
                in_plane(which, 2 * k).wait_send()
                in_plane(which, 2 * k + 1).wait_send()
    drain_halo(0, 0)
    for q in range(chunks):
        drain_halo(1, q)
        for j in range(tiles):
            core_copy(q, j).wait_send()
            y_copy(q, j).wait_send()
    for slot in range(slots):
        if slot != HOME:
            for j in range(tiles):
                z_copy(slot, j).wait_send()


def shards(pos_factor, vel_factor, stiff_vals, stiff_pattern, mass_vals, mass_pattern, interface):
    wide, narrow = lax.axis_size("wide"), lax.axis_size("narrow")
    cols = pos_factor.shape[0]
    dofs = pos_factor.shape[1] // wide
    every = cols * wide
    slots = len(SHIFTS)
    chunks = len(CUTS) - 1
    rows = max(hi - lo for lo, hi in zip(CUTS, CUTS[1:])) * cols
    tiles = every // TILE
    extended = dofs + 2 * LANES
    scale = 1.0 / math.sqrt(dofs * wide * narrow)
    f32, b16 = jnp.float32, jnp.bfloat16
    vmem = functools.partial(pl.BlockSpec, memory_space=pltpu.VMEM)
    smem = functools.partial(pl.BlockSpec, memory_space=pltpu.SMEM)
    hbm = functools.partial(pl.BlockSpec, memory_space=pl.ANY)
    dma = pltpu.SemaphoreType.DMA
    return pl.pallas_call(
        functools.partial(kernel, scale),
        out_shape=jax.ShapeDtypeStruct((8, every), f32),
        in_specs=[hbm(), hbm(), vmem(), smem(), vmem(), smem(), smem()],
        out_specs=vmem(),
        scratch_shapes=[
            pltpu.VMEM((slots, cols, dofs), f32),
            pltpu.VMEM((slots, cols, dofs), f32),
            pltpu.VMEM((2, len(PAIRS), cols, dofs), f32),
            pltpu.VMEM((2, 2, slots, cols, LANES), f32),
            pltpu.VMEM((2, 2, slots, cols, LANES), f32),
            pltpu.VMEM((dofs, extended), b16),
            pltpu.VMEM((dofs, extended), b16),
            pltpu.VMEM((dofs, extended), b16),
            pltpu.VMEM((dofs, extended), b16),
            pltpu.VMEM((every, extended), b16),
            pltpu.VMEM((every, extended), b16),
            pltpu.VMEM((every, extended), b16),
            pltpu.VMEM((every, extended), b16),
            pltpu.VMEM((every, dofs), f32),
            pltpu.VMEM((rows, dofs), f32),
            pltpu.VMEM((rows, dofs), b16),
            pltpu.VMEM((rows, dofs), b16),
            pltpu.VMEM((every, dofs), b16),
            pltpu.VMEM((every, dofs), b16),
            pltpu.VMEM((2, tiles, slots, 2, 8, TILE), f32),
            pltpu.VMEM((tiles, slots, 2, 8, TILE), f32),
            pltpu.VMEM((2, tiles, slots, 8, TILE), f32),
            pltpu.VMEM((tiles, slots, 8, TILE), f32),
            pltpu.VMEM((slots, 8, every), f32),
            pltpu.VMEM((slots, 8, every), f32),
            dma((2, slots)), dma((2, slots)), dma((2,)),
            dma((2, len(PAIRS))), dma((2, len(PAIRS))),
            dma((1 + chunks, 2)), dma((1 + chunks, 2)),
            dma((chunks, tiles)), dma((chunks, tiles)),
            dma((chunks, tiles)), dma((chunks, tiles)),
            dma((slots, tiles)), dma((slots, tiles)),
        ],
        compiler_params=pltpu.CompilerParams(
            collective_id=0, has_side_effects=True, vmem_limit_bytes=63 << 20
        ),
    )(
        pos_factor, vel_factor, stiff_vals, jnp.swapaxes(stiff_pattern, 1, 2),
        mass_vals, jnp.swapaxes(mass_pattern, 1, 2), interface,
    )


def solution(mesh):
    return jax.shard_map(
        shards,
        mesh=mesh,
        in_specs=(
            P("wide", "narrow"),
            P("wide", "narrow"),
            P("narrow", "wide", None, None),
            P("narrow", "wide", None),
            P("narrow", "wide", None, None),
            P("narrow", "wide", None),
            P("narrow", "wide", None, None),
        ),
        out_specs=P(("wide", "narrow"), None),
        check_vma=False,
    )
```

time: 958 us -> 161 us (0.17)
  waiting for transfers between devices: 756 us -> 0 us
  Pallas kernels: 0 us -> 160 us
  local copies, waits for them, and re-layouts: 91.5 us -> 1.38 us
  matrix products: 66.8 us -> 0 us
  starting transfers between devices: 20.2 us -> 0 us
  between operations: 13.7 us -> 0.01 us
    reduce_scatter x1 -> x0, waiting for transfers between devices: 663 us -> none  [shards(): lax.psum_scatter(product * scale, ('wide', 'narrow'), scatter_dimension=0...]
    pallas_call x0 -> x1, Pallas kernels: none -> 160 us  [shards(): pl.pallas_call(functools.partial(kernel, scale), out_shape=jax.ShapeDtype...]
    all_to_all x2 -> x0, waiting for transfers between devices: 87.3 us -> none  [the longest x1 52.1 us: shards(): lax.all_to_all(pos_factor, 'wide', split_axis=1, concat_axis=0, tiled=True)]
    dot_general x9 -> x0, matrix products: 66.8 us -> none  [the longest x8 44.3 us: apply_block_matrix(): jnp.einsum('rbj,bij->rbi', picked, coupled, precision=lax.Precision.HIGHEST)]
    gather x12 -> x0, local copies, waits for them, and re-layouts: 53.4 us -> none  [the longest x8 42.3 us: apply_block_matrix(): picked = jnp.take(extended, pattern[:, k], axis=1)]
    reshape x4 -> x0, local copies, waits for them, and re-layouts: 28.2 us -> none  [as_blocks(): return field.reshape(field.shape[0], block_count, block_size)]
    all_to_all x2 -> x0, starting transfers between devices: 17.3 us -> none  [the longest x1 9.41 us: shards(): lax.all_to_all(pos_factor, 'wide', split_axis=1, concat_axis=0, tiled=True)]
  transfers between devices with their start and end apart: 5 -> 0, of which waited for: 5 -> 0; matrix products, arithmetic and copies ran while one was open for 3% -> 0% of each run, Pallas kernels for 0% -> 0%
where the time goes in v2:
time: 161 us
  Pallas kernels  160 us (99%)
    pallas_call x1, Pallas kernels, shards(): pl.pallas_call(functools.partial(kernel, scale), out_shape=jax.ShapeDtype...  160 us

profile of v2, /device:TPU:0, one launch (start us, length us, event | category | flops | bytes accessed | tf_op | source)
XLA Modules:
  0.0 161.0 jit_solution(12803693803033158717)
XLA Ops:
  0.0 159.6 %shard_map.73 = f32[8,1024]{1,0:T(8,128)} custom-call(f32[32,32768]{1,0:T(8,128)} %pos_ref.1, f32[32,32768]{1,0:T(8,128)} %vel_ref.1, f32[1,16,64,256]{3,2,1,0:T(8,128)} %stiff_ref.1, s32[1,4,16]{2,1,0:T(4,128)} %bitcast.2, f32[1,16,64,256]{3,2,1,0:T(8,128)} %mass_ref.1, s32[1,4,16]{2,1,0:T(4,128)} %bitcast.3, s32[1,1,2,2]{3,2,1,0:T(2,128)} %picks.1), custom_call_target="tpu_custom_call" | custom-call | tf_op jit(solution)/shard_map/pallas_call | solution.py:460
  159.6 1.4 copy.9

commit v3 on v2

--- a/solution.py
+++ b/solution.py
@@ -21,7 +21,7 @@
 )
 SHIFTS = tuple((dy, dx, dz) for dx, dz in PAIRS for dy in (0, 1))
 CUTS = (0, 8, 16, 24, 32)
-WINDOW = 8
+WINDOW = 6
 LAG = 5
 TILE = 256
 HOME = SHIFTS.index((0, 0, 0))
@@ -198,32 +198,44 @@
         for way in range(2):
             halo_out[which, way, entry] = found[way]
 
-    def halo_copy(which, q, way):
-        lo, hi = (0, slots) if which == 0 else CUTS[q:q + 2]
-        n = 0 if which == 0 else 1 + q
+    def halo_copy(which, n, way, view):
         return pltpu.make_async_remote_copy(
-            src_ref=halo_out.at[which, way, lo:hi], dst_ref=halo.at[which, way, lo:hi],
+            src_ref=halo_out.at[which, way, view], dst_ref=halo.at[which, way, view],
             send_sem=halo_send.at[n, way], recv_sem=halo_recv.at[n, way],
             device_id={"narrow": (narrow + (1 if way == 0 else 3)) % 4}, device_id_type=MESH,
         )
+
+    def halo_copies(which, q, way):
+        if which == 0:
+            return [halo_copy(0, slot, way, slice(slot, slot + 1)) for slot in range(slots)]
+        return [halo_copy(1, slots + q, way, slice(*CUTS[q:q + 2]))]
+
+    def send_block_halo(slot, entry):
+        for way in range(2):
+            @pl.when(narrow != (3 if way == 0 else 0))
+            def _():
+                halo_copy(0, slot, way, pl.ds(entry, 1)).start()
 
     def send_halo(which, q):
         for way in range(2):
             @pl.when(narrow != (3 if way == 0 else 0))
             def _():
-                halo_copy(which, q, way).start()
+                for copy in halo_copies(which, q, way):
+                    copy.start()
 
     def take_halo(which, q):
         for way in range(2):
             @pl.when(narrow != (0 if way == 0 else 3))
             def _():
-                halo_copy(which, q, way).wait_recv()
+                for copy in halo_copies(which, q, way):
+                    copy.wait_recv()
 
     def drain_halo(which, q):
         for way in range(2):
             @pl.when(narrow != (3 if way == 0 else 0))
             def _():
-                halo_copy(which, q, way).wait_send()
+                for copy in halo_copies(which, q, way):
+                    copy.wait_send()
 
     def per_tile(count, body):
         def one(j, carry):
@@ -364,6 +376,7 @@
             arrived(0, slot)
             source = source_of(slot)
             take_in(0, vel_in, source, ev_h, ev_l, pl.ds(pl.multiple_of(source * cols, cols), cols))
+            send_block_halo(slot, source)
 
     pending = list(range(2 * pairs))
 
@@ -381,7 +394,6 @@
     for k in range(pairs):
         steps(1)
         velocity_in(k)
-    send_halo(0, 0)
     for q in range(every // TILE):
         velocity_first(q)
         steps(1)
@@ -490,7 +502,7 @@
             pltpu.VMEM((slots, 8, every), f32),
             dma((2, slots)), dma((2, slots)), dma((2,)),
             dma((2, len(PAIRS))), dma((2, len(PAIRS))),
-            dma((1 + chunks, 2)), dma((1 + chunks, 2)),
+            dma((slots + chunks, 2)), dma((slots + chunks, 2)),
             dma((chunks, tiles)), dma((chunks, tiles)),
             dma((chunks, tiles)), dma((chunks, tiles)),
             dma((slots, tiles)), dma((slots, tiles)),

time: 161 us -> 161 us (level); the launches traced: 161 us -> 159 us
  Pallas kernels: 160 us -> 157 us
    pallas_call x1, Pallas kernels: 160 us -> 157 us  [shards(): pl.pallas_call(functools.partial(kernel, scale), out_shape=jax.ShapeDtype...]
where the time goes in v3:
time: 161 us; the launch traced here: 159 us
  Pallas kernels  157 us (98%)
    pallas_call x1, Pallas kernels, shards(): pl.pallas_call(functools.partial(kernel, scale), out_shape=jax.ShapeDtype...  157 us

profile of v3, /device:TPU:0, one launch (start us, length us, event | category | flops | bytes accessed | tf_op | source)
XLA Modules:
  0.0 158.9 jit_solution(9176226958674996044)
XLA Ops:
  0.0 157.5 %shard_map.73 = f32[8,1024]{1,0:T(8,128)} custom-call(f32[32,32768]{1,0:T(8,128)} %pos_ref.1, f32[32,32768]{1,0:T(8,128)} %vel_ref.1, f32[1,16,64,256]{3,2,1,0:T(8,128)} %stiff_ref.1, s32[1,4,16]{2,1,0:T(4,128)} %bitcast.2, f32[1,16,64,256]{3,2,1,0:T(8,128)} %mass_ref.1, s32[1,4,16]{2,1,0:T(4,128)} %bitcast.3, s32[1,1,2,2]{3,2,1,0:T(2,128)} %picks.1), custom_call_target="tpu_custom_call" | custom-call | tf_op jit(solution)/shard_map/pallas_call | solution.py:472
  157.5 1.4 copy.9
